TPU v7x, 256 devices: a whole 4x4x8 slice. The times are simulated.
256 devices in a mesh: row: 8 (over z_hi, x), col: 32 (over y, z_lo, core).
Axes of the slice: x: 4, y: 4, z: 8 (z_hi: 2, z_lo: 4; z = z_hi * 4 + z_lo), core: 2. Of those that a mesh axis runs over, the one named last changes fastest.
Arguments:
- prior_cov: float32 [16384, 16384], P('row', 'col'), as said below
- diffusivity: float32 [16384], replicated, may hold values from 0.05 to 0.2
- velocity: float32 [2, 16384], replicated, may hold values from -0.3 to 0.3
- process_noise_variance: float32 [16384], replicated, may hold values from 0.2 to 1
- observed_index: int32 [256], replicated, may hold values from 0 to 16383, as said below
- innov_factor: float32 [256, 256], replicated, may hold values from -0.048 to 1.048
Outputs:
- analysis_cov: float32 [16384, 16384], P('row', 'col')
Inputs may be any that keep to these rules, and one draw needn't show every extreme that they name: `prior_cov`: symmetric positive definite. `observed_index`: 256 distinct point indices.
All inputs are finite; a program needn't handle non-finite values.
Results may differ from a plain program's by a relative error of at most 0.000098.
Values sent between devices are 32-bit elements; how exact they have to be, the bound alone decides.
A program may use at most 128 MiB of HBM per device.

v0:
```python
import jax
import jax.numpy as jnp
from jax import lax
from jax.sharding import PartitionSpec as P

GY = 128
STEPS = 2


def with_halo(shard, sides, width):
    for axis, dim in sides:
        peers, length = (lax.axis_size(axis), shard.shape[dim])
        up = [(i, (i + 1) % peers) for i in range(peers - 1)]
        down = [(j, i) for i, j in up]
        last = lax.slice_in_dim(shard, length - width, length, axis=dim)
        leading = lax.slice_in_dim(shard, 0, width, axis=dim)
        before = lax.ppermute(last, axis, up)
        after = lax.ppermute(leading, axis, down)
        shard = jnp.concatenate([before, shard, after], axis=dim)
    return shard


def advect(values, diffuse_coef, east_speed, south_speed, grid_axis):
    extent = values.shape[grid_axis]
    north_side = lax.slice_in_dim(values, 0, extent - 2, axis=grid_axis)
    center = lax.slice_in_dim(values, 1, extent - 1, axis=grid_axis)
    south_side = lax.slice_in_dim(values, 2, extent, axis=grid_axis)
    span_cols = values.shape[grid_axis + 1]
    zero_edge = jnp.zeros_like(lax.slice_in_dim(center, 0, 1, axis=grid_axis + 1))
    east_side = jnp.concatenate(
        [lax.slice_in_dim(center, 1, span_cols, axis=grid_axis + 1), zero_edge], axis=grid_axis + 1
    )
    west_side = jnp.concatenate(
        [zero_edge, lax.slice_in_dim(center, 0, span_cols - 1, axis=grid_axis + 1)],
        axis=grid_axis + 1,
    )
    laplace = north_side + south_side + east_side + west_side - 4.0 * center
    return (
        center
        + diffuse_coef * laplace
        - 0.5 * east_speed * (east_side - west_side)
        - 0.5 * south_speed * (south_side - north_side)
    )


def on_device(
    prior_cov, diffusivity, velocity, process_noise_variance, observed_index, innov_factor
):
    top_precision = lax.Precision.HIGHEST
    rows_dev, cols_dev = prior_cov.shape
    row_start = lax.axis_index("row") * rows_dev
    col_start = lax.axis_index("col") * cols_dev
    margin = GY * STEPS
    diffuse_pad = jnp.pad(diffusivity, (margin, margin))
    east_pad = jnp.pad(velocity[0], (margin, margin))
    south_pad = jnp.pad(velocity[1], (margin, margin))

    def window(offset, amount, shaped):
        return tuple(
            (
                lax.dynamic_slice_in_dim(table, offset + margin, amount).reshape(shaped)
                for table in (diffuse_pad, east_pad, south_pad)
            )
        )

    present_state = prior_cov
    coefs = window(row_start, rows_dev, (rows_dev // GY, GY, 1))
    for substep in range(STEPS):
        widened = with_halo(present_state, (("row", 0),), GY)
        present_state = advect(
            widened.reshape(-1, GY, cols_dev), coefs[0], coefs[1], coefs[2], 0
        ).reshape(rows_dev, cols_dev)
    coefs = window(col_start, cols_dev, (1, cols_dev // GY, GY))
    for substep in range(STEPS):
        widened = with_halo(present_state, (("col", 1),), GY)
        present_state = advect(
            widened.reshape(rows_dev, -1, GY), coefs[0], coefs[1], coefs[2], 1
        ).reshape(rows_dev, cols_dev)
    row_labels = row_start + lax.iota(jnp.int32, rows_dev)
    column_labels = col_start + lax.iota(jnp.int32, cols_dev)
    variance_rows = lax.dynamic_slice_in_dim(process_noise_variance, row_start, rows_dev)
    predicted_cov = present_state + jnp.where(
        row_labels[:, None] == column_labels[None, :], variance_rows[:, None], 0.0
    )
    pick_cols = (column_labels[:, None] == observed_index[None, :]).astype(jnp.float32)
    pick_rows = (row_labels[:, None] == observed_index[None, :]).astype(jnp.float32)
    stencil_weights = jnp.dot(
        pick_cols, innov_factor.T, precision=top_precision, preferred_element_type=jnp.float32
    )
    partial_left_product = jnp.dot(
        predicted_cov, stencil_weights, precision=top_precision, preferred_element_type=jnp.float32
    )
    left_multiplier = lax.psum(partial_left_product, "col")
    observed = lax.dot_general(
        pick_rows,
        predicted_cov,
        (((0,), (0,)), ((), ())),
        precision=top_precision,
        preferred_element_type=jnp.float32,
    )
    observed = lax.psum(observed, "row")
    right_multiplier = jnp.dot(
        innov_factor, observed, precision=top_precision, preferred_element_type=jnp.float32
    )
    return predicted_cov - jnp.dot(
        left_multiplier,
        right_multiplier,
        precision=top_precision,
        preferred_element_type=jnp.float32,
    )


def solution(mesh):
    return jax.shard_map(
        on_device,
        mesh=mesh,
        in_specs=(P("row", "col"), P(), P(), P(), P(), P()),
        out_specs=P("row", "col"),
        check_vma=False,
    )
```

profile of v0, /device:TPU:1, one launch (start us, length us, event | category | flops | bytes accessed | tf_op | source)
XLA Modules:
  0.0 592.9 jit_solution(15418751431844451939)
XLA Ops:
  7.6 3.9 collective-permute-start
  14.0 5.4 copy.11
  19.4 7.9 %fusion.39 = (f32[16,127,512]{1,0,2:T(8,128)}, f32[16,127,512]{1,0,2:T(8,128)}) fusion(f32[16,128,512]{1,0,2:T(8,128)} %copy.11), kind=kLoop, calls=%fused_computation.66 | loop fusion | bytes 16646144 | tf_op jit(solution)/shard_map/slice | solution.py:31
  27.5 7.7 %fusion.6 = (f32[2048,512]{1,0:T(8,128)}, f32[2048,512]{1,0:T(8,128)}) fusion(f32[2048,512]{1,0:T(8,128)} %param.6, f32[128,512]{1,0:T(8,128)S(1)} %collective-permute-done, f32[128,512]{1,0:T(8,128)S(1)} %collective-permute-done.1), kind=kLoop, calls=%fused_computation.22 | loop fusion | flops 4194304 | bytes 13107200 | tf_op jit(solution)/shard_map/add | solution.py:37
  35.2 5.4 copy.12
  40.6 5.4 copy.8
  46.1 8.1 %multiply_subtract_fusion.2 = f32[16,128,512]{1,0,2:T(8,128)S(1)} fusion(f32[16,128,512]{1,0,2:T(8,128)} %copy.12, f32[16,128,512]{1,0,2:T(8,128)} %copy.11, f32[16,127,512]{1,0,2:T(8,128)} %get-tuple-element.22, f32[16,128,512]{1,0,2:T(8,128)} %copy.8, f32[16,127,512]{1,0,2:T(8,128)} %get-tuple-element.21, f32[16,128]{1,0:T(8,128)S(1)} %fusion.29, ...), kind=kLoop, calls=%fused_computation.21 | loop fusion | flops 11534336 | bytes 25124864 | tf_op jit(solution)/shard_map/sub | solution.py:39
  54.5 4.0 collective-permute-start.2
  60.0 3.4 fusion.37
  63.4 2.0 copy.22
  71.0 2.7 fusion
  73.7 2.0 copy.21
  75.7 2.0 copy-done.1
  78.9 5.8 collective-permute-start.4
  84.7 2.1 collective-permute-start.5
  87.7 13.6 %collective-permute-done.4 = f32[2048,128]{0,1:T(8,128)S(1)} collective-permute-done((f32[2048,128]{0,1:T(8,128)}, f32[2048,128]{0,1:T(8,128)S(1)}, u32[]{:S(2)}, u32[]{:S(2)}) %collective-permute-start.4) | collective-permute-done | bytes 1048608 | tf_op jit(solution)/shard_map/ppermute | solution.py:17
  101.4 8.0 %collective-permute-done.5 = f32[2048,128]{0,1:T(8,128)S(1)} collective-permute-done((f32[2048,128]{0,1:T(8,128)S(1)}, f32[2048,128]{0,1:T(8,128)S(1)}, u32[]{:S(2)}, u32[]{:S(2)}) %collective-permute-start.5) | collective-permute-done | bytes 1048608 | tf_op jit(solution)/shard_map/ppermute | solution.py:18
  109.4 2.6 pad_maximum_fusion
  113.2 2.7 multiply_subtract_fusion.1
  115.9 2.0 copy-done.2
  121.0 2.5 collective-permute-start.7
  124.2 8.8 %collective-permute-done.6 = f32[2048,128]{0,1:T(8,128)S(1)} collective-permute-done((f32[2048,128]{0,1:T(8,128)}, f32[2048,128]{0,1:T(8,128)S(1)}, u32[]{:S(2)}, u32[]{:S(2)}) %collective-permute-start.6) | collective-permute-done | bytes 1048608 | tf_op jit(solution)/shard_map/ppermute | solution.py:17
  133.1 17.9 %collective-permute-done.7 = f32[2048,128]{0,1:T(8,128)S(1)} collective-permute-done((f32[2048,128]{0,1:T(8,128)S(1)}, f32[2048,128]{0,1:T(8,128)S(1)}, u32[]{:S(2)}, u32[]{:S(2)}) %collective-permute-start.7) | collective-permute-done | bytes 1048608 | tf_op jit(solution)/shard_map/ppermute | solution.py:18
  151.0 2.6 pad_maximum_fusion.1
  154.8 4.1 multiply_subtract_fusion
  159.0 5.3 copy.14
  164.3 6.1 %fusion.8 = f32[256,512]{1,0:T(8,128)} fusion(f32[2048,512]{1,0:T(8,128)} %copy.14, f32[2048]{0:T(1024)S(1)} %dynamic_slice.27, s32[512]{0:T(512)S(1)} %iota_add_fusion.1, s32[2048]{0:T(1024)S(1)} %iota_add_fusion, s32[256]{0:T(256)S(1)} %copy-done.5), kind=kOutput, calls=%fused_computation.25 | convolution fusion | flops 3224895488 | bytes 4738048 | tf_op jit(solution)/shard_map/dot_general | solution.py:94
  171.2 7.2 %fusion.9 = f32[2048,256]{1,0:T(8,128)} fusion(f32[512,256]{1,0:T(8,128)S(1)} %fusion.21, f32[2048,512]{1,0:T(8,128)} %copy.14, f32[2048]{0:T(1024)S(1)} %dynamic_slice.27, s32[512]{0:T(512)S(1)} %iota_add_fusion.1, s32[2048]{0:T(1024)S(1)} %iota_add_fusion), kind=kOutput, calls=%fused_computation.26 | convolution fusion | flops 3224371200 | bytes 6834176 | tf_op jit(solution)/shard_map/dot_general | solution.py:90
  178.4 111.9 %all-reduce.16.cloned.1.call-done = f32[256,512]{1,0:T(8,128)} async-done(((f32[256,512]{1,0:T(8,128)}), f32[256,512]{1,0:T(8,128)}) %all-reduce.16.cloned.1.call-update) | async-done | bytes 524304 | tf_op jit(solution)/shard_map/psum | solution.py:101
  290.3 2.0 fusion.42
  292.4 285.0 %all-reduce.14.cloned.1.call-done = f32[2048,256]{1,0:T(8,128)} async-done(((f32[2048,256]{1,0:T(8,128)}), f32[2048,256]{1,0:T(8,128)}) %all-reduce.14.cloned.1.call-update) | async-done | bytes 2097168 | tf_op jit(solution)/shard_map/psum | solution.py:93
  577.4 8.7 %convolution_subtract_fusion = f32[2048,512]{1,0:T(8,128)} fusion(f32[2048,256]{1,0:T(8,128)} %all-reduce.14.cloned.1.call-done, f32[512,256]{1,0:T(8,128)S(1)} %fusion.42, f32[2048,512]{1,0:T(8,128)} %copy.14, f32[2048]{0:T(1024)S(1)} %dynamic_slice.27, s32[512]{0:T(512)S(1)} %iota_add_fusion.1, s32[2048]{0:T(1024)S(1)} %iota_add_fusion), kind=kOutput, calls=%fused_computation.24 | convolution fusion | flops 3225419776 | bytes 11028480 | tf_op jit(solution)/shard_map/dot_general | solution.py:105
  (39 shorter events, 20.2 us)
Async XLA Ops:
  6.5 164.2 %copy-start = (f32[256,256]{1,0:T(8,128)S(1)}, f32[256,256]{1,0:T(8,128)}, u32[]{:S(2)}) copy-start(f32[256,256]{1,0:T(8,128)} %param.11) | copy-start | bytes 786436
  6.5 283.8 %all-reduce.16.cloned.1.call-start = ((), (), s32[]{:S(2)}) async-start(), calls=%async_computation.1 | async-start | bytes 1048576 | tf_op jit(solution)/shard_map/psum | solution.py:101
  7.6 19.9 %collective-permute-start = (f32[128,512]{1,0:T(8,128)S(1)}, f32[128,512]{1,0:T(8,128)S(1)}, u32[]{:S(2)}, u32[]{:S(2)}) collective-permute-start(f32[128,512]{1,0:T(8,128)S(1)} %get-tuple-element.24), channel_id=1, source_target_pairs={{0,32},{32,64},{64,96},{96,128},{128,160},{160,192},{192,224},{1,3... | collective-permute-start | bytes 786440 | tf_op jit(solution)/shard_map/ppermute | solution.py:17
  11.6 15.9 %collective-permute-start.1 = (f32[128,512]{1,0:T(8,128)S(1)}, f32[128,512]{1,0:T(8,128)S(1)}, u32[]{:S(2)}, u32[]{:S(2)}) collective-permute-start(f32[128,512]{1,0:T(8,128)S(1)} %get-tuple-element.23), channel_id=1, source_target_pairs={{32,0},{64,32},{96,64},{128,96},{160,128},{192,160},{224,192},{33,... | collective-permute-start | bytes 786440 | tf_op jit(solution)/shard_map/ppermute | solution.py:18
  19.4 8.0 %copy-start.4 = (f32[16384]{0:T(1024)S(1)}, f32[16384]{0:T(1024)}, u32[]{:S(2)}) copy-start(f32[16384]{0:T(1024)} %param.7) | copy-start | bytes 196612
  54.5 10.8 %collective-permute-start.2 = (f32[128,512]{0,1:T(8,128)S(1)}, f32[128,512]{0,1:T(8,128)S(1)}, u32[]{:S(2)}, u32[]{:S(2)}) collective-permute-start(f32[128,512]{0,1:T(8,128)S(1)} %bitcast.87), channel_id=1, source_target_pairs={{0,32},{32,64},{64,96},{96,128},{128,160},{160,192},{192,224},{1,3... | collective-permute-start | bytes 786440 | tf_op jit(solution)/shard_map/ppermute | solution.py:17
  58.5 8.2 %collective-permute-start.3 = (f32[128,512]{0,1:T(8,128)S(1)}, f32[128,512]{0,1:T(8,128)S(1)}, u32[]{:S(2)}, u32[]{:S(2)}) collective-permute-start(f32[128,512]{0,1:T(8,128)S(1)} %bitcast.86), channel_id=1, source_target_pairs={{32,0},{64,32},{96,64},{128,96},{160,128},{192,160},{224,192},{33,... | collective-permute-start | bytes 786440 | tf_op jit(solution)/shard_map/ppermute | solution.py:18
  68.8 2.2 copy-start.3
  75.7 2.0 copy-start.1
  78.9 22.5 %collective-permute-start.4 = (f32[2048,128]{0,1:T(8,128)}, f32[2048,128]{0,1:T(8,128)S(1)}, u32[]{:S(2)}, u32[]{:S(2)}) collective-permute-start(f32[2048,128]{0,1:T(8,128)} %get-tuple-element.15), channel_id=1, source_target_pairs={{0,1},{1,2},{2,3},{3,4},{4,5},{5,6},{6,7},{7,8},{8,9},{9,10},{10,1... | collective-permute-start | bytes 3145736 | tf_op jit(solution)/shard_map/ppermute | solution.py:17
  84.7 24.6 %collective-permute-start.5 = (f32[2048,128]{0,1:T(8,128)S(1)}, f32[2048,128]{0,1:T(8,128)S(1)}, u32[]{:S(2)}, u32[]{:S(2)}) collective-permute-start(f32[2048,128]{0,1:T(8,128)S(1)} %get-tuple-element.16), channel_id=1, source_target_pairs={{1,0},{2,1},{3,2},{4,3},{5,4},{6,5},{7,6},{8,7},{9,8},{10,9},{11,1... | collective-permute-start | bytes 3145736 | tf_op jit(solution)/shard_map/ppermute | solution.py:18
  115.9 2.0 copy-start.2
  119.1 14.0 %collective-permute-start.6 = (f32[2048,128]{0,1:T(8,128)}, f32[2048,128]{0,1:T(8,128)S(1)}, u32[]{:S(2)}, u32[]{:S(2)}) collective-permute-start(f32[2048,128]{0,1:T(8,128)} %get-tuple-element.13), channel_id=1, source_target_pairs={{0,1},{1,2},{2,3},{3,4},{4,5},{5,6},{6,7},{7,8},{8,9},{9,10},{10,1... | collective-permute-start | bytes 3145736 | tf_op jit(solution)/shard_map/ppermute | solution.py:17
  121.0 30.0 %collective-permute-start.7 = (f32[2048,128]{0,1:T(8,128)S(1)}, f32[2048,128]{0,1:T(8,128)S(1)}, u32[]{:S(2)}, u32[]{:S(2)}) collective-permute-start(f32[2048,128]{0,1:T(8,128)S(1)} %get-tuple-element.14), channel_id=1, source_target_pairs={{1,0},{2,1},{3,2},{4,3},{5,4},{6,5},{7,6},{8,7},{9,8},{10,9},{11,1... | collective-permute-start | bytes 3145736 | tf_op jit(solution)/shard_map/ppermute | solution.py:18
  159.0 5.3 copy-start.5
  170.4 406.9 %all-reduce.14.cloned.1.call-start = ((), (), s32[]{:S(2)}) async-start(), calls=%async_computation | async-start | bytes 4194304 | tf_op jit(solution)/shard_map/psum | solution.py:93
Sparse Core Ops, SparseCore 0:
  170.6 119.7 all-reduce.15
  292.9 284.3 all-reduce.13
where the time goes:
time: 594 us; the launch traced here: 593 us
  waiting for transfers between devices  447 us (75%)
  local copies, waits for them, and re-layouts  52.8 us (9%)
  other arithmetic  31.9 us (5%)
  matrix products  24.5 us (4%)
  starting transfers between devices  23.3 us (4%)
  between operations  13.6 us (2%)
    psum x1, waiting for transfers between devices, on_device(): left_multiplier = lax.psum(partial_left_product, 'col')  285 us
    psum x1, waiting for transfers between devices, on_device(): observed = lax.psum(observed, 'row')  112 us
    ppermute x4, waiting for transfers between devices, with_halo(): after = lax.ppermute(leading, axis, down)  27.3 us
    ppermute x4, waiting for transfers between devices, with_halo(): before = lax.ppermute(last, axis, up)  22.5 us
    sub x4, other arithmetic, advect(): center + diffuse_coef * laplace - 0.5 * east_speed * (east_side - west_side)  17.6 us
    ppermute x4, starting transfers between devices, with_halo(): before = lax.ppermute(last, axis, up)  15.7 us
    slice x4, local copies, waits for them, and re-layouts, advect(): lax.slice_in_dim(center, 1, span_cols, axis=grid_axis + 1)  13.7 us
  transfers between devices with their start and end apart: 10, of which 7 were waited for; matrix products, arithmetic and copies ran while one was open for 5% of the time, Pallas kernels for 0%

commit v1 on v0

--- a/solution.py
+++ b/solution.py
@@ -98,7 +98,7 @@
         precision=top_precision,
         preferred_element_type=jnp.float32,
     )
-    observed = lax.psum(observed, "row")
+    observed = jnp.sum(lax.all_gather(observed, "row"), axis=0)
     right_multiplier = jnp.dot(
         innov_factor, observed, precision=top_precision, preferred_element_type=jnp.float32
     )

time: 594 us -> 545 us (0.918)
  waiting for transfers between devices: 447 us -> 395 us
    psum x1 -> x0, waiting for transfers between devices: 112 us -> none  [on_device(): observed = lax.psum(observed, 'row')]
    all_gather x0 -> x1, waiting for transfers between devices: none -> 101 us  [on_device(): observed = jnp.sum(lax.all_gather(observed, 'row'), axis=0)]
    psum x1, waiting for transfers between devices: 285 us -> 244 us  [on_device(): left_multiplier = lax.psum(partial_left_product, 'col')]
  transfers between devices with their start and end apart: 10 -> 10, of which waited for: 7 -> 7; matrix products, arithmetic and copies ran while one was open for 5% -> 6% of each run, Pallas kernels for 0% -> 0%
where the time goes in v1:
time: 545 us; the launch traced here: 544 us
  waiting for transfers between devices  395 us (72%)
  local copies, waits for them, and re-layouts  52.8 us (10%)
  other arithmetic  34.6 us (6%)
  matrix products  23.4 us (4%)
  starting transfers between devices  23.3 us (4%)
  between operations  15.1 us (3%)
    psum x1, waiting for transfers between devices, on_device(): left_multiplier = lax.psum(partial_left_product, 'col')  244 us
    all_gather x1, waiting for transfers between devices, on_device(): observed = jnp.sum(lax.all_gather(observed, 'row'), axis=0)  101 us
    ppermute x4, waiting for transfers between devices, with_halo(): after = lax.ppermute(leading, axis, down)  27.3 us
    ppermute x4, waiting for transfers between devices, with_halo(): before = lax.ppermute(last, axis, up)  22.5 us
    sub x4, other arithmetic, advect(): center + diffuse_coef * laplace - 0.5 * east_speed * (east_side - west_side)  17.6 us
    ppermute x4, starting transfers between devices, with_halo(): before = lax.ppermute(last, axis, up)  15.7 us
    slice x4, local copies, waits for them, and re-layouts, advect(): lax.slice_in_dim(center, 1, span_cols, axis=grid_axis + 1)  13.7 us
    unnamed x16, local copies, waits for them, and re-layouts  11 us
  transfers between devices with their start and end apart: 10, of which 7 were waited for; matrix products, arithmetic and copies ran while one was open for 6% of the time, Pallas kernels for 0%

profile of v1, /device:TPU:1, one launch (start us, length us, event | category | flops | bytes accessed | tf_op | source)
XLA Modules:
  0.0 544.3 jit_solution(3032923433871870497)
XLA Ops:
  8.5 3.9 collective-permute-start
  14.8 5.4 copy.11
  20.3 7.9 %fusion.39 = (f32[16,127,512]{1,0,2:T(8,128)}, f32[16,127,512]{1,0,2:T(8,128)}) fusion(f32[16,128,512]{1,0,2:T(8,128)} %copy.11), kind=kLoop, calls=%fused_computation.66 | loop fusion | bytes 16646144 | tf_op jit(solution)/shard_map/slice | solution.py:31
  28.3 7.7 %fusion.6 = (f32[2048,512]{1,0:T(8,128)}, f32[2048,512]{1,0:T(8,128)}) fusion(f32[2048,512]{1,0:T(8,128)} %param.6, f32[128,512]{1,0:T(8,128)S(1)} %collective-permute-done, f32[128,512]{1,0:T(8,128)S(1)} %collective-permute-done.1), kind=kLoop, calls=%fused_computation.22 | loop fusion | flops 4194304 | bytes 13107200 | tf_op jit(solution)/shard_map/add | solution.py:37
  36.0 5.4 copy.12
  41.5 5.4 copy.8
  46.9 8.1 %multiply_subtract_fusion.2 = f32[16,128,512]{1,0,2:T(8,128)S(1)} fusion(f32[16,128,512]{1,0,2:T(8,128)} %copy.12, f32[16,128,512]{1,0,2:T(8,128)} %copy.11, f32[16,127,512]{1,0,2:T(8,128)} %get-tuple-element.22, f32[16,128,512]{1,0,2:T(8,128)} %copy.8, f32[16,127,512]{1,0,2:T(8,128)} %get-tuple-element.21, f32[16,128]{1,0:T(8,128)S(1)} %fusion.29, ...), kind=kLoop, calls=%fused_computation.21 | loop fusion | flops 11534336 | bytes 25124864 | tf_op jit(solution)/shard_map/sub | solution.py:39
  55.3 4.0 collective-permute-start.2
  60.8 3.4 fusion.37
  64.2 2.0 copy.22
  71.8 2.7 fusion
  74.6 2.0 copy.21
  76.5 2.0 copy-done.1
  79.8 5.8 %collective-permute-start.4 = (f32[2048,128]{0,1:T(8,128)}, f32[2048,128]{0,1:T(8,128)S(1)}, u32[]{:S(2)}, u32[]{:S(2)}) collective-permute-start(f32[2048,128]{0,1:T(8,128)} %get-tuple-element.15), channel_id=1, source_target_pairs={{0,1},{1,2},{2,3},{3,4},{4,5},{5,6},{6,7},{7,8},{8,9},{9,10},{10,1... | collective-permute-start | bytes 3145736 | tf_op jit(solution)/shard_map/ppermute | solution.py:17
  85.6 2.1 collective-permute-start.5
  88.6 13.6 %collective-permute-done.4 = f32[2048,128]{0,1:T(8,128)S(1)} collective-permute-done((f32[2048,128]{0,1:T(8,128)}, f32[2048,128]{0,1:T(8,128)S(1)}, u32[]{:S(2)}, u32[]{:S(2)}) %collective-permute-start.4) | collective-permute-done | bytes 1048608 | tf_op jit(solution)/shard_map/ppermute | solution.py:17
  102.2 8.0 %collective-permute-done.5 = f32[2048,128]{0,1:T(8,128)S(1)} collective-permute-done((f32[2048,128]{0,1:T(8,128)S(1)}, f32[2048,128]{0,1:T(8,128)S(1)}, u32[]{:S(2)}, u32[]{:S(2)}) %collective-permute-start.5) | collective-permute-done | bytes 1048608 | tf_op jit(solution)/shard_map/ppermute | solution.py:18
  110.2 2.6 pad_maximum_fusion
  114.0 2.7 multiply_subtract_fusion.1
  116.8 2.0 copy-done.2
  121.9 2.5 collective-permute-start.7
  125.1 8.8 %collective-permute-done.6 = f32[2048,128]{0,1:T(8,128)S(1)} collective-permute-done((f32[2048,128]{0,1:T(8,128)}, f32[2048,128]{0,1:T(8,128)S(1)}, u32[]{:S(2)}, u32[]{:S(2)}) %collective-permute-start.6) | collective-permute-done | bytes 1048608 | tf_op jit(solution)/shard_map/ppermute | solution.py:17
  133.9 17.9 %collective-permute-done.7 = f32[2048,128]{0,1:T(8,128)S(1)} collective-permute-done((f32[2048,128]{0,1:T(8,128)S(1)}, f32[2048,128]{0,1:T(8,128)S(1)}, u32[]{:S(2)}, u32[]{:S(2)}) %collective-permute-start.7) | collective-permute-done | bytes 1048608 | tf_op jit(solution)/shard_map/ppermute | solution.py:18
  151.8 2.6 pad_maximum_fusion.1
  155.7 4.1 multiply_subtract_fusion
  159.8 5.3 copy.14
  165.1 6.1 %fusion.8 = f32[256,512]{1,0:T(8,128)} fusion(f32[2048,512]{1,0:T(8,128)} %copy.14, f32[2048]{0:T(1024)S(1)} %dynamic_slice.27, s32[512]{0:T(512)S(1)} %iota_add_fusion.1, s32[2048]{0:T(1024)S(1)} %iota_add_fusion, s32[256]{0:T(256)S(1)} %copy-done.5), kind=kOutput, calls=%fused_computation.25 | convolution fusion | flops 3224895488 | bytes 4738048 | tf_op jit(solution)/shard_map/dot_general | solution.py:94
  172.0 7.2 %fusion.9 = f32[2048,256]{1,0:T(8,128)} fusion(f32[512,256]{1,0:T(8,128)S(1)} %fusion.21, f32[2048,512]{1,0:T(8,128)} %copy.14, f32[2048]{0:T(1024)S(1)} %dynamic_slice.27, s32[512]{0:T(512)S(1)} %iota_add_fusion.1, s32[2048]{0:T(1024)S(1)} %iota_add_fusion), kind=kOutput, calls=%fused_computation.26 | convolution fusion | flops 3224371200 | bytes 6834176 | tf_op jit(solution)/shard_map/dot_general | solution.py:90
  179.3 101.2 %all-gather.3.cloned.1.call-done = f32[2048,512]{1,0:T(8,128)} async-done(((f32[256,512]{1,0:T(8,128)}), f32[2048,512]{1,0:T(8,128)}) %all-gather.3.cloned.1.call-update) | async-done | bytes 4194320 | tf_op jit(solution)/shard_map/all_gather | solution.py:101
  280.4 2.7 reduce_sum.9
  284.2 244.0 %all-reduce.13.cloned.1.call-done = f32[2048,256]{1,0:T(8,128)} async-done(((f32[2048,256]{1,0:T(8,128)}), f32[2048,256]{1,0:T(8,128)}) %all-reduce.13.cloned.1.call-update) | async-done | bytes 2097168 | tf_op jit(solution)/shard_map/psum | solution.py:93
  528.2 8.7 %convolution_subtract_fusion = f32[2048,512]{1,0:T(8,128)} fusion(f32[2048,256]{1,0:T(8,128)} %all-reduce.13.cloned.1.call-done, f32[512,256]{1,0:T(8,128)S(1)} %fusion.42, f32[2048,512]{1,0:T(8,128)} %copy.14, f32[2048]{0:T(1024)S(1)} %dynamic_slice.27, s32[512]{0:T(512)S(1)} %iota_add_fusion.1, s32[2048]{0:T(1024)S(1)} %iota_add_fusion), kind=kOutput, calls=%fused_computation.24 | convolution fusion | flops 3225419776 | bytes 11028480 | tf_op jit(solution)/shard_map/dot_general | solution.py:105
  (40 shorter events, 21.2 us)
Async XLA Ops:
  7.4 164.2 %copy-start = (f32[256,256]{1,0:T(8,128)S(1)}, f32[256,256]{1,0:T(8,128)}, u32[]{:S(2)}) copy-start(f32[256,256]{1,0:T(8,128)} %param.11) | copy-start | bytes 786436
  7.4 273.1 %all-gather.3.cloned.1.call-start = ((), (), s32[]{:S(2)}) async-start(), calls=%async_computation.1 | async-start | bytes 4718592 | tf_op jit(solution)/shard_map/all_gather | solution.py:101
  8.5 19.9 %collective-permute-start = (f32[128,512]{1,0:T(8,128)S(1)}, f32[128,512]{1,0:T(8,128)S(1)}, u32[]{:S(2)}, u32[]{:S(2)}) collective-permute-start(f32[128,512]{1,0:T(8,128)S(1)} %get-tuple-element.24), channel_id=1, source_target_pairs={{0,32},{32,64},{64,96},{96,128},{128,160},{160,192},{192,224},{1,3... | collective-permute-start | bytes 786440 | tf_op jit(solution)/shard_map/ppermute | solution.py:17
  12.4 15.9 %collective-permute-start.1 = (f32[128,512]{1,0:T(8,128)S(1)}, f32[128,512]{1,0:T(8,128)S(1)}, u32[]{:S(2)}, u32[]{:S(2)}) collective-permute-start(f32[128,512]{1,0:T(8,128)S(1)} %get-tuple-element.23), channel_id=1, source_target_pairs={{32,0},{64,32},{96,64},{128,96},{160,128},{192,160},{224,192},{33,... | collective-permute-start | bytes 786440 | tf_op jit(solution)/shard_map/ppermute | solution.py:18
  20.3 8.0 %copy-start.4 = (f32[16384]{0:T(1024)S(1)}, f32[16384]{0:T(1024)}, u32[]{:S(2)}) copy-start(f32[16384]{0:T(1024)} %param.7) | copy-start | bytes 196612
  55.3 10.8 %collective-permute-start.2 = (f32[128,512]{0,1:T(8,128)S(1)}, f32[128,512]{0,1:T(8,128)S(1)}, u32[]{:S(2)}, u32[]{:S(2)}) collective-permute-start(f32[128,512]{0,1:T(8,128)S(1)} %bitcast.89), channel_id=1, source_target_pairs={{0,32},{32,64},{64,96},{96,128},{128,160},{160,192},{192,224},{1,3... | collective-permute-start | bytes 786440 | tf_op jit(solution)/shard_map/ppermute | solution.py:17
  59.3 8.2 %collective-permute-start.3 = (f32[128,512]{0,1:T(8,128)S(1)}, f32[128,512]{0,1:T(8,128)S(1)}, u32[]{:S(2)}, u32[]{:S(2)}) collective-permute-start(f32[128,512]{0,1:T(8,128)S(1)} %bitcast.88), channel_id=1, source_target_pairs={{32,0},{64,32},{96,64},{128,96},{160,128},{192,160},{224,192},{33,... | collective-permute-start | bytes 786440 | tf_op jit(solution)/shard_map/ppermute | solution.py:18
  69.7 2.2 copy-start.3
  76.5 2.0 copy-start.1
  79.8 22.5 %collective-permute-start.4 = (f32[2048,128]{0,1:T(8,128)}, f32[2048,128]{0,1:T(8,128)S(1)}, u32[]{:S(2)}, u32[]{:S(2)}) collective-permute-start(f32[2048,128]{0,1:T(8,128)} %get-tuple-element.15), channel_id=1, source_target_pairs={{0,1},{1,2},{2,3},{3,4},{4,5},{5,6},{6,7},{7,8},{8,9},{9,10},{10,1... | collective-permute-start | bytes 3145736 | tf_op jit(solution)/shard_map/ppermute | solution.py:17
  85.6 24.6 %collective-permute-start.5 = (f32[2048,128]{0,1:T(8,128)S(1)}, f32[2048,128]{0,1:T(8,128)S(1)}, u32[]{:S(2)}, u32[]{:S(2)}) collective-permute-start(f32[2048,128]{0,1:T(8,128)S(1)} %get-tuple-element.16), channel_id=1, source_target_pairs={{1,0},{2,1},{3,2},{4,3},{5,4},{6,5},{7,6},{8,7},{9,8},{10,9},{11,1... | collective-permute-start | bytes 3145736 | tf_op jit(solution)/shard_map/ppermute | solution.py:18
  116.7 2.0 copy-start.2
  120.0 14.0 %collective-permute-start.6 = (f32[2048,128]{0,1:T(8,128)}, f32[2048,128]{0,1:T(8,128)S(1)}, u32[]{:S(2)}, u32[]{:S(2)}) collective-permute-start(f32[2048,128]{0,1:T(8,128)} %get-tuple-element.13), channel_id=1, source_target_pairs={{0,1},{1,2},{2,3},{3,4},{4,5},{5,6},{6,7},{7,8},{8,9},{9,10},{10,1... | collective-permute-start | bytes 3145736 | tf_op jit(solution)/shard_map/ppermute | solution.py:17
  121.9 30.0 %collective-permute-start.7 = (f32[2048,128]{0,1:T(8,128)S(1)}, f32[2048,128]{0,1:T(8,128)S(1)}, u32[]{:S(2)}, u32[]{:S(2)}) collective-permute-start(f32[2048,128]{0,1:T(8,128)S(1)} %get-tuple-element.14), channel_id=1, source_target_pairs={{1,0},{2,1},{3,2},{4,3},{5,4},{6,5},{7,6},{8,7},{9,8},{10,9},{11,1... | collective-permute-start | bytes 3145736 | tf_op jit(solution)/shard_map/ppermute | solution.py:18
  159.8 5.3 copy-start.5
  171.3 356.9 %all-reduce.13.cloned.1.call-start = ((), (), s32[]{:S(2)}) async-start(), calls=%async_computation | async-start | bytes 4194304 | tf_op jit(solution)/shard_map/psum | solution.py:93
Sparse Core Ops, SparseCore 0:
  171.4 108.9 all-gather.2
Sparse Core Ops, SparseCore 1:
  179.3 348.8 all-reduce.12
